TPU v7x, 128 devices: a whole 4x4x4 slice. The times are simulated.
128 devices in a mesh: dp: 16 (over z, x), head: 8 (over y, core).
Axes of the slice: x: 4, y: 4, z: 4, core: 2. Of those that a mesh axis runs over, the one named last changes fastest.
Arguments:
- prefill_query: bfloat16 [16384, 8192], P(('dp', 'head')), may hold values from -20 to 20
- prefill_pairs: bfloat16 [16384, 2048], P(('dp', 'head')), may hold values from -4 to 4
- decode_query: bfloat16 [128, 8192], P(('dp', 'head')), may hold values from -20 to 20
- decode_pairs: bfloat16 [128, 2048], P(('dp', 'head')), may hold values from -4 to 4
- cache_pool: bfloat16 [2560, 8, 64, 256], P('dp', 'head'), may hold values from -11 to 11
- decode_pages: int32 [128, 16], P('dp'), may hold values from 0 to 159, as said below
- prefill_pages: int32 [16, 32], P('dp'), may hold values from 0 to 159, as said below
- cache_length: int32 [128], replicated, may hold values from 1 to 1023, as said below
- prefix_length: int32 [16], P('dp'), may hold values from 0 to 1024, as said below
- migrant_slot: int32 [16, 1], replicated, may hold values from 0 to 7, as said below
- migrant_target: int32 [16, 1], replicated, may hold values from 0 to 15, as said below
- arrivals: int32 [128], replicated, may hold values from 0 to 127, each once
Outputs:
- prefill_attended: bfloat16 [16384, 8192], P(('dp', 'head'))
- decode_attended: bfloat16 [128, 8192], P('dp', 'head')
- updated_pool: bfloat16 [2560, 8, 64, 256], P('dp', 'head')
Inputs may be any that keep to these rules, and one draw needn't show every extreme that they name: Page numbers within the group's pool; in each group the entries of its 8 rows of decode_pages and its row of prefill_pages are all different. `prefill_pages`: see decode_pages. `cache_length`: A migrating request holds at most 255 cached tokens, and one holds exactly 255. `prefix_length`: A multiple of 64. `migrant_slot`: the slots of one group are all different. `migrant_target`: each column is a permutation of the groups: every group receives exactly one request of each column; a request may stay in its group.
All inputs are finite; a program needn't handle non-finite values.
Results may differ from a plain program's by a relative error of at most 0.008.
Values may be sent and summed in bfloat16 or wider, within the bound.
A program may use at most 128 MiB of HBM per device.

v0:
```python
import jax
import jax.numpy as jnp
from jax import lax
from jax.sharding import PartitionSpec as P

HD = 128
PAGE = 64
MIGP = 4
big_negative = -1e30


def decode_attend(queries, key_pages, lengths, inv_scale):
    slot_count = queries.shape[0]
    local_heads = key_pages.shape[2]
    page_size = key_pages.shape[3]
    head_size = key_pages.shape[4] // 2
    per_group = queries.shape[1] // (local_heads * head_size)
    grouped = queries.reshape(slot_count, local_heads, per_group, head_size)
    scores = (
        jnp.einsum(
            "skqd,smkpd->skqmp",
            grouped,
            key_pages[..., :head_size],
            preferred_element_type=jnp.float32,
        )
        * inv_scale
    )
    position = (
        jnp.arange(key_pages.shape[1], dtype=jnp.int32)[:, None] * page_size
        + jnp.arange(page_size, dtype=jnp.int32)[None, :]
    )
    visible = position[None, None, None] <= lengths[:, None, None, None, None]
    masked = jnp.where(visible, scores, big_negative)
    row_top = jnp.max(masked, axis=(3, 4), keepdims=True)
    weights = jnp.where(visible, jnp.exp(masked - row_top), 0.0)
    weight_sum = jnp.sum(weights, axis=(3, 4))
    mixed_sum = jnp.einsum(
        "skqmp,smkpd->skqd",
        weights.astype(jnp.bfloat16),
        key_pages[..., head_size:],
        preferred_element_type=jnp.float32,
    )
    return (mixed_sum / weight_sum[..., None]).reshape(slot_count, -1).astype(jnp.bfloat16)


def prefill_block(queries, key_pages, limit, inv_scale):
    row_total = queries.shape[0]
    local_heads = key_pages.shape[1]
    page_size = key_pages.shape[2]
    head_size = key_pages.shape[3] // 2
    per_group = queries.shape[1] // (local_heads * head_size)
    grouped = queries.reshape(row_total, local_heads, per_group, head_size)
    scores = (
        jnp.einsum(
            "tkqd,mkpd->kqtmp",
            grouped,
            key_pages[..., :head_size],
            preferred_element_type=jnp.float32,
        )
        * inv_scale
    )
    position = (
        jnp.arange(key_pages.shape[0], dtype=jnp.int32)[:, None] * page_size
        + jnp.arange(page_size, dtype=jnp.int32)[None, :]
    )
    visible = position[None, None, None] <= limit[None, None, :, None, None]
    masked = jnp.where(visible, scores, big_negative)
    row_top = jnp.max(masked, axis=(3, 4), keepdims=True)
    weights = jnp.where(visible, jnp.exp(masked - row_top), 0.0)
    weight_sum = jnp.sum(weights, axis=(3, 4))
    mixed_sum = jnp.einsum(
        "kqtmp,mkpd->tkqd",
        weights.astype(jnp.bfloat16),
        key_pages[..., head_size:],
        preferred_element_type=jnp.float32,
    )
    return (
        (mixed_sum / weight_sum.transpose(2, 0, 1)[..., None])
        .reshape(row_total, -1)
        .astype(jnp.bfloat16)
    )


def per_device(
    prefill_query,
    prefill_pairs,
    decode_query,
    decode_pairs,
    cache_pool,
    decode_pages,
    prefill_pages,
    cache_length,
    prefix_length,
    migrant_slot,
    migrant_target,
    arrivals,
):
    inv_scale = HD ** (-0.5)
    my_group = lax.axis_index("dp")
    head_part = lax.axis_index("head")
    slot_count = decode_pages.shape[0]
    mig_count = migrant_slot.shape[1]
    local_heads = cache_pool.shape[1]
    query_width = decode_query.shape[1] // lax.axis_size("head")
    pair_width = decode_pairs.shape[1] // lax.axis_size("head")
    my_slots = migrant_slot[my_group]
    own_pages = decode_pages[my_slots][:, :MIGP]
    leaving = cache_pool[own_pages]
    flat_target = migrant_target.reshape(-1)
    shard_piece = lax.all_gather(leaving, "dp", axis=0, tiled=True)
    row_count = shard_piece.shape[0]
    row_index = jnp.arange(row_count, dtype=jnp.int32)
    chosen = jnp.logical_and(
        (flat_target == my_group)[:, None],
        (row_index % mig_count)[:, None] == jnp.arange(mig_count, dtype=jnp.int32)[None, :],
    )
    moved_pages = jnp.einsum(
        "nk,nabcd->kabcd",
        chosen.astype(jnp.bfloat16),
        shard_piece,
        preferred_element_type=jnp.float32,
    )
    arriving = moved_pages.astype(jnp.bfloat16)
    new_pool = cache_pool.at[own_pages.reshape(-1)].set(
        arriving.reshape((-1,) + cache_pool.shape[1:])
    )
    source_slot = (
        jnp.arange(migrant_target.shape[0], dtype=jnp.int32)[:, None] * slot_count + migrant_slot
    )
    incoming_len = jnp.sum(
        jnp.where(migrant_target == my_group, cache_length[source_slot], 0), axis=0
    )
    own_len = lax.dynamic_slice_in_dim(cache_length, my_group * slot_count, slot_count)
    lengths = own_len.at[my_slots].set(incoming_len)
    wanted = my_group * slot_count + jnp.arange(slot_count, dtype=jnp.int32)
    onehot = (wanted[:, None] == arrivals[None, :]).astype(jnp.bfloat16)
    query_cols = lax.dynamic_slice_in_dim(
        lax.all_gather(decode_query, ("dp", "head"), axis=0, tiled=True),
        head_part * query_width,
        query_width,
        1,
    )
    pair_cols = lax.dynamic_slice_in_dim(
        lax.all_gather(decode_pairs, ("dp", "head"), axis=0, tiled=True),
        head_part * pair_width,
        pair_width,
        1,
    )
    query_rows = jnp.dot(onehot, query_cols, preferred_element_type=jnp.float32)
    pair_rows = jnp.dot(onehot, pair_cols, preferred_element_type=jnp.float32)
    query_rows = query_rows.astype(jnp.bfloat16)
    pair_rows = pair_rows.astype(jnp.bfloat16)
    page_index = lengths // PAGE
    page_now = jnp.take_along_axis(decode_pages, page_index[:, None], axis=1)[:, 0]
    new_pool = new_pool.at[page_now, :, lengths % PAGE, :].set(
        pair_rows.reshape(slot_count, local_heads, 2 * HD)
    )
    decode_attended = decode_attend(query_rows, new_pool[decode_pages], lengths, inv_scale)
    query_all, pair_all = (
        lax.all_to_all(prefill_query, "head", split_axis=1, concat_axis=0, tiled=True),
        lax.all_to_all(prefill_pairs, "head", split_axis=1, concat_axis=0, tiled=True),
    )
    span_rows = query_all.shape[0]
    pre_table = prefill_pages[0]
    prefix = prefix_length[0]
    span_pages = pair_all.reshape(span_rows // PAGE, PAGE, local_heads, 2 * HD).transpose(
        0, 2, 1, 3
    )
    dest_pages = lax.dynamic_slice_in_dim(pre_table, prefix // PAGE, span_rows // PAGE)
    new_pool = new_pool.at[dest_pages].set(span_pages)
    key_pages = new_pool[pre_table]
    block_rows = min(128, span_rows)
    blocks = query_all.reshape(span_rows // block_rows, block_rows, query_width)
    limits = (prefix + jnp.arange(span_rows, dtype=jnp.int32)).reshape(
        span_rows // block_rows, block_rows
    )

    def attend_block(block_items):
        return prefill_block(block_items[0], key_pages, block_items[1], inv_scale)

    outputs = lax.map(attend_block, (blocks, limits))
    out_span = outputs.reshape(span_rows, query_width)
    prefill_attended = lax.all_to_all(out_span, "head", split_axis=0, concat_axis=1, tiled=True)
    return (prefill_attended, decode_attended, new_pool)


def solution(mesh):
    placed = (
        P(("dp", "head"), None),
        P(("dp", "head"), None),
        P(("dp", "head"), None),
        P(("dp", "head"), None),
        P("dp", "head", None, None),
        P("dp", None),
        P("dp", None),
        P(),
        P("dp"),
        P(),
        P(),
        P(),
    )
    return jax.shard_map(
        per_device,
        mesh=mesh,
        in_specs=placed,
        out_specs=(P(("dp", "head"), None), P("dp", "head"), P("dp", "head", None, None)),
        check_vma=False,
    )
```

profile of v0, /device:TPU:1, one launch (start us, length us, event | category | flops | bytes accessed | tf_op | source)
XLA Modules:
  0.0 207.4 jit_solution(15597287813363803023)
XLA Ops:
  7.3 5.8 %copy.75 = bf16[160,1,64,256]{3,2,1,0:T(8,128)(2,1)} copy(bf16[160,1,64,256]{3,2,1,0:T(8,128)(2,1)} %param.20) | data formatting | bytes 10485760
  13.1 0.6 compare_select_fusion.9
  13.8 0.7 constant_dynamic-slice_fusion.2
  14.5 3.7 %gather_fusion = bf16[4,64,256]{2,1,0:T(8,128)(2,1)} fusion(bf16[160,64,256]{2,1,0:T(8,128)(2,1)} %bitcast.221, s32[1024]{0:T(1024)S(1)} %pad_clamp_fusion.3), kind=kCustom, calls=%fused_computation | custom fusion | bytes 262160 | tf_op jit(solution)/shard_map/gather | solution.py:108
  18.2 0.8 copy.59
  19.0 6.1 %all-to-all-start.1 = ((bf16[128,8,256]{2,0,1:T(8,128)(2,1)}), bf16[128,8,256]{2,0,1:T(8,128)(2,1)S(1)}, u32[]{:S(2)}, u32[]{:S(2)}) async-start(bf16[128,8,256]{2,0,1:T(8,128)(2,1)} %bitcast.188), calls=%async_computation.1 | async-start | bytes 1048576 | tf_op jit(solution)/shard_map/all_to_all | solution.py:161
  25.1 0.7 all-gather.8.cloned.1.call-update
  26.6 0.7 gather_fusion.1
  27.3 0.7 fusion.52
  28.0 2.1 %fusion.61 = s32[8]{0:T(128)S(1)} fusion(s32[8]{0:T(128)S(1)} %dynamic_slice.28, s32[]{:T(128)} %bitcast.25, s32[1]{0:T(128)} %bitcast.36, s32[128]{0:T(128)S(1)} %copy-done, s32[]{:T(128)S(6)} %dynamic_slice.29, s32[1,1]{0,1:T(1,128)} %get-tuple-element.67), kind=kLoop, calls=%fused_computation.116 | loop fusion | flops 7 | bytes 560 | tf_op jit(solution)/shard_map/scatter | solution.py:134
  31.0 2.5 %copy.24 = bf16[128,8192]{0,1:T(8,128)(2,1)} copy(bf16[128,8192]{1,0:T(8,128)(2,1)S(1)} %copy-done.2) | data formatting | bytes 4194304 | tf_op args[0]
  33.5 1.1 all-to-all-done.1
  34.6 4.4 %all-to-all-start = ((bf16[128,8,1024]{0,2,1:T(8,128)(2,1)}), bf16[128,8,1024]{0,2,1:T(8,128)(2,1)S(1)}, u32[]{:S(2)}, u32[]{:S(2)}) async-start(bf16[128,8,1024]{0,2,1:T(8,128)(2,1)} %bitcast.21), calls=%async_computation | async-start | bytes 4194304 | tf_op jit(solution)/shard_map/all_to_all | solution.py:160
  39.1 0.6 gather_fusion.4
  39.8 55.8 %all-gather.1 = bf16[128,1,2048]{2,1,0:T(2,128)(2,1)S(1)} all-gather(bf16[1,1,2048]{2,1,0:T(2,128)(2,1)S(1)} %bitcast.237), channel_id=1, replica_groups=mesh['dp'=16,'head'=8] {'dp','head'}, dimensions={0}, use_global_device_ids=true | all-gather | bytes 528384 | tf_op jit(solution)/shard_map/all_gather | solution.py:144
  95.9 2.9 %fusion.27 = bf16[1,4,64,256]{3,0,2,1:T(2,128)(2,1)S(1)} fusion(bf16[16,4,64,256]{3,2,1,0:T(8,128)(2,1)} %bitcast.230, s32[16,1]{0,1:T(1,128)S(1)} %copy-done.5, s32[]{:T(128)S(6)} %axis_index.23), kind=kOutput, calls=%fused_computation.38 | convolution fusion | flops 2097168 | bytes 2228292 | tf_op jit(solution)/shard_map/nk,nabcd->kabcd/dot_general | solution.py:117
  98.8 2.0 scatter_fusion
  100.8 2.1 %scatter_fusion.1 = bf16[160,64,256]{2,1,0:T(8,128)(2,1)} fusion(bf16[160,64,256]{2,1,0:T(8,128)(2,1)} %scatter_fusion, s32[8]{0:T(128)S(1)} %fusion.62, bf16[8,256]{1,0:T(8,128)(2,1)S(1)} %convolution_convert_fusion.1), kind=kCustom, calls=%fused_computation.6 | custom fusion | bytes 12352 | tf_op jit(solution)/shard_map/scatter | solution.py:155
  102.9 5.3 %gather_fusion.3 = bf16[128,64,256]{2,1,0:T(8,128)(2,1)} fusion(bf16[160,64,256]{2,1,0:T(8,128)(2,1)} %scatter_fusion.1, s32[1024]{0:T(1024)S(1)} %pad_clamp_fusion), kind=kCustom, calls=%fused_computation.3 | custom fusion | bytes 8389120 | tf_op jit(solution)/shard_map/gather | solution.py:158
  108.2 2.6 %scatter_fusion.2 = bf16[160,64,256]{2,1,0:T(8,128)(2,1)} fusion(bf16[160,64,256]{2,1,0:T(8,128)(2,1)} %scatter_fusion.1, s32[16]{0:T(128)S(1)} %fusion.60, bf16[16,64,256]{2,1,0:T(8,128)(2,1)S(1)} %bitcast.231), kind=kCustom, calls=%fused_computation.7 | custom fusion | bytes 1572928 | tf_op jit(solution)/shard_map/scatter | solution.py:170
  110.8 3.1 %gather_fusion.2 = bf16[32,64,256]{2,1,0:T(8,128)(2,1)S(1)} fusion(bf16[160,64,256]{2,1,0:T(8,128)(2,1)} %scatter_fusion.2, s32[1024]{0:T(1024)S(1)} %pad_clamp_fusion.1), kind=kCustom, calls=%fused_computation.2 | custom fusion | bytes 2097280 | tf_op jit(solution)/shard_map/gather | solution.py:171
  113.9 53.5 %while.12 = (s32[]{:T(128)}, bf16[8,128,1024]{1,2,0:T(8,128)(2,1)}, s32[8,128]{1,0:T(8,128)S(1)}, bf16[8,128,1024]{1,2,0:T(8,128)(2,1)S(1)}, bf16[32,1,64,256]{3,2,0,1:T(8,128)(2,1)S(1)}, /*index=5*/s32[]{:T(128)}) while((s32[]{:T(128)}, bf16[8,128,1024]{1,2,0:T(8,128)(2,1)}, s32[8,128]{1,0:T(8,128)S(1)}, bf16[8,128,1024]{1,2,0:T(8,128)(2,1)S(1)}, ...), condition=%wide.region_7.8_spmd, body=%wide.region_4.7_spmd.sunk | while | flops 1101529088 | bytes 28875084 | solution.py:181
  114.0 0.3 broadcast_compare_fusion.3
  114.4 1.4 fusion.79
  115.7 2.0 fusion.80
  117.8 2.1 fusion.81
  119.9 0.7 constant_dynamic-update-slice_fusion.2
  121.0 1.4 fusion.79
  122.4 2.0 fusion.80
  124.5 2.1 fusion.81
  126.5 0.7 constant_dynamic-update-slice_fusion.2
  127.3 0.3 broadcast_compare_fusion.3
  127.7 1.4 fusion.79
  129.1 2.0 fusion.80
  131.1 2.1 fusion.81
  133.2 0.7 constant_dynamic-update-slice_fusion.2
  134.0 0.3 broadcast_compare_fusion.3
  134.4 1.4 fusion.79
  135.8 2.0 fusion.80
  137.8 2.1 fusion.81
  139.9 0.7 constant_dynamic-update-slice_fusion.2
  141.1 1.4 fusion.79
  142.5 2.0 fusion.80
  144.5 2.1 fusion.81
  146.6 0.7 constant_dynamic-update-slice_fusion.2
  147.8 1.4 fusion.79
  149.2 2.0 fusion.80
  151.2 2.1 fusion.81
  153.3 0.7 constant_dynamic-update-slice_fusion.2
  154.5 1.4 fusion.79
  155.8 2.0 fusion.80
  157.9 2.1 fusion.81
  159.9 0.7 constant_dynamic-update-slice_fusion.2
  161.1 1.4 fusion.79
  162.5 2.0 fusion.80
  164.6 2.1 fusion.81
  166.6 0.7 constant_dynamic-update-slice_fusion.2
  167.4 4.0 %all-to-all-start.2 = ((bf16[8,128,1024]{1,2,0:T(8,128)(2,1)}), bf16[8,128,1024]{1,2,0:T(8,128)(2,1)S(1)}, u32[]{:S(2)}, u32[]{:S(2)}) async-start(bf16[8,128,1024]{1,2,0:T(8,128)(2,1)} %get-tuple-element.42), calls=%async_computation.2 | async-start | bytes 4194304 | tf_op jit(solution)/shard_map/all_to_all | solution.py:183
  171.6 1.6 constant_dynamic-slice_fusion.3
  173.4 3.4 %fusion.65 = (f32[8,8]{1,0:T(8,128)S(1)}, f32[8,8,16,64]{3,1,2,0:T(8,128)S(1)}) fusion(bf16[8,16,1,64,256]{4,3,1,0,2:T(8,128)(2,1)} %bitcast.225, bf16[8,8,128,1]{2,0,1,3:T(8,128)(2,1)S(1)} %fusion.32, pred[8,16,64]{2,1,0:T(8,128)(4,1)S(1)} %broadcast_compare_fusion.1), kind=kOutput, calls=%fused_computation.120 | convolution fusion | flops 16973760 | bytes 2384128 | tf_op jit(solution)/shard_map/skqd,smkpd->skqmp/dot_general | solution.py:20
  177.1 2.2 %fusion.35 = bf16[1,8,8,128]{3,2,1,0:T(8,128)(2,1)S(1)} fusion(bf16[8,16,1,64,256]{4,3,1,0,2:T(8,128)(2,1)} %bitcast.226, f32[8,8,16,64]{3,1,2,0:T(8,128)S(1)} %get-tuple-element.69, f32[8,8]{1,0:T(8,128)S(1)} %get-tuple-element.68, pred[8,16,64]{2,1,0:T(8,128)(4,1)S(1)} %broadcast_compare_fusion.1, f32[8,8]{1,0:T(8,128)S(1)} %fusion.36), kind=kOutput, calls=%fused_computation.48 | convolution fusion | flops 16990208 | bytes 2384384 | tf_op jit(solution)/shard_map/skqmp,smkpd->skqd/dot_general | solution.py:37
  179.2 0.6 copy.61
  179.9 17.9 %all-to-all-done.2 = bf16[8,128,1024]{1,2,0:T(8,128)(2,1)S(1)} async-done(((bf16[8,128,1024]{1,2,0:T(8,128)(2,1)}), bf16[8,128,1024]{1,2,0:T(8,128)(2,1)S(1)}, u32[]{:S(2)}, u32[]{:S(2)}) %all-to-all-start.2) | async-done | bytes 2097184 | tf_op jit(solution)/shard_map/all_to_all | solution.py:183
  197.7 2.9 %copy.39 = bf16[128,8192]{1,0:T(8,128)(2,1)} copy(bf16[128,8192]{0,1:T(8,128)(2,1)S(1)} %bitcast.227) | data formatting | bytes 4194304 | tf_op jit(solution)/shard_map/all_to_all | solution.py:183
  (89 shorter events, 4.0 us)
Async XLA Ops:
  7.2 23.8 %copy-start.2 = (bf16[128,8192]{1,0:T(8,128)(2,1)S(1)}, bf16[128,8192]{1,0:T(8,128)(2,1)}, u32[]{:S(2)}) copy-start(bf16[128,8192]{1,0:T(8,128)(2,1)} %param.16) | copy-start | bytes 6291460
  7.2 11.0 %copy-start.3 = (bf16[128,2048]{1,0:T(8,128)(2,1)S(1)}, bf16[128,2048]{1,0:T(8,128)(2,1)}, u32[]{:S(2)}) copy-start(bf16[128,2048]{1,0:T(8,128)(2,1)} %param.17) | copy-start | bytes 1572868
  7.2 6.6 %copy-start.1 = (s32[8,16]{1,0:T(8,128)S(1)}, s32[8,16]{1,0:T(8,128)}, u32[]{:S(2)}) copy-start(s32[8,16]{1,0:T(8,128)} %param.21) | copy-start | bytes 1540
  7.2 19.3 %copy-start = (s32[128]{0:T(128)S(1)}, s32[128]{0:T(128)}, u32[]{:S(2)}) copy-start(s32[128]{0:T(128)} %param.23) | copy-start | bytes 1540
  7.2 5.9 %copy-start.6 = (s32[16,1]{0,1:T(1,128)S(1)}, s32[16,1]{0,1:T(1,128)}, u32[]{:S(2)}) copy-start(s32[16,1]{0,1:T(1,128)} %param.25) | copy-start | bytes 196
  7.2 20.1 %copy-start.5 = (s32[16,1]{0,1:T(1,128)S(1)}, s32[16,1]{0,1:T(1,128)}, u32[]{:S(2)}) copy-start(s32[16,1]{0,1:T(1,128)} %param.26) | copy-start | bytes 196
  7.2 88.7 %all-gather.6.cloned.1.call-start = ((), (), s32[]{:S(2)}) async-start(), calls=%async_computation.3 | async-start | bytes 2228224 | tf_op jit(solution)/shard_map/all_gather | solution.py:110
  19.0 20.0 %copy-start.7 = (s32[1,32]{1,0:T(1,128)S(1)}, s32[1,32]{1,0:T(1,128)}, u32[]{:S(2)}) copy-start(s32[1,32]{1,0:T(1,128)} %param.22) | copy-start | bytes 388
  19.0 20.7 %copy-start.4 = (bf16[1,2048]{1,0:T(2,128)(2,1)S(1)}, bf16[1,2048]{1,0:T(2,128)(2,1)}, u32[]{:S(2)}) copy-start(bf16[1,2048]{1,0:T(2,128)(2,1)} %param.19) | copy-start | bytes 12292
  19.0 15.6 %all-to-all-start.1 = ((bf16[128,8,256]{2,0,1:T(8,128)(2,1)}), bf16[128,8,256]{2,0,1:T(8,128)(2,1)S(1)}, u32[]{:S(2)}, u32[]{:S(2)}) async-start(bf16[128,8,256]{2,0,1:T(8,128)(2,1)} %bitcast.188), calls=%async_computation.1 | async-start | bytes 1048576 | tf_op jit(solution)/shard_map/all_to_all | solution.py:161
  25.1 146.5 %all-gather.8.cloned.1.call-start = ((), (), s32[]{:S(2)}) async-start(), calls=%async_computation.4 | async-start | bytes 4227072 | tf_op jit(solution)/shard_map/all_gather | solution.py:138
  27.3 68.4 %copy-start.8 = (s32[128]{0:T(128)S(1)}, s32[128]{0:T(128)}, u32[]{:S(2)}) copy-start(s32[128]{0:T(128)} %param.27) | copy-start | bytes 1540
  34.6 79.3 %all-to-all-start = ((bf16[128,8,1024]{0,2,1:T(8,128)(2,1)}), bf16[128,8,1024]{0,2,1:T(8,128)(2,1)S(1)}, u32[]{:S(2)}, u32[]{:S(2)}) async-start(bf16[128,8,1024]{0,2,1:T(8,128)(2,1)} %bitcast.21), calls=%async_computation | async-start | bytes 4194304 | tf_op jit(solution)/shard_map/all_to_all | solution.py:160
  167.4 30.4 %all-to-all-start.2 = ((bf16[8,128,1024]{1,2,0:T(8,128)(2,1)}), bf16[8,128,1024]{1,2,0:T(8,128)(2,1)S(1)}, u32[]{:S(2)}, u32[]{:S(2)}) async-start(bf16[8,128,1024]{1,2,0:T(8,128)(2,1)} %get-tuple-element.42), calls=%async_computation.2 | async-start | bytes 4194304 | tf_op jit(solution)/shard_map/all_to_all | solution.py:183
Sparse Core Ops, SparseCore 0:
  18.3 47.4 all-gather.5
  68.9 67.5 all-gather.7
where the time goes:
time: 208 us; the launch traced here: 207 us
  blocking collectives  55.8 us (27%)
  local copies, waits for them, and re-layouts  41.3 us (20%)
  matrix products  36.4 us (18%)
  other arithmetic  23.6 us (11%)
  waiting for transfers between devices  19.8 us (10%)
  between operations  15.6 us (8%)
  starting transfers between devices  14.6 us (7%)
    all_gather x1, blocking collectives, per_device(): lax.all_gather(decode_pairs, ('dp', 'head'), axis=0, tiled=True)  55.8 us
    all_to_all x1, waiting for transfers between devices, per_device(): lax.all_to_all(out_span, 'head', split_axis=0, concat_axis=1, tiled=True)  17.9 us
    dot_general x8, matrix products, prefill_block(): jnp.einsum('kqtmp,mkpd->tkqd', weights.astype(jnp.bfloat16), key_pages[.....  16.6 us
    reduce_sum x8, other arithmetic, prefill_block(): weight_sum = jnp.sum(weights, axis=(3, 4))  16.2 us
    dot_general x8, matrix products, prefill_block(): jnp.einsum('tkqd,mkpd->kqtmp', grouped, key_pages[..., :head_size], prefe...  11 us
    unnamed x22, local copies, waits for them, and re-layouts  8.98 us
    all_to_all x1, starting transfers between devices, per_device(): lax.all_to_all(prefill_pairs, 'head', split_axis=1, concat_axis=0, tiled=...  6.1 us
    dynamic_update_slice x8, local copies, waits for them, and re-layouts, per_device(): outputs = lax.map(attend_block, (blocks, limits))  5.81 us
  transfers between devices with their start and end apart: 5, of which 2 were waited for; matrix products, arithmetic and copies ran while one was open for 42% of the time, Pallas kernels for 0%

commit v1 on v0

--- a/solution.py
+++ b/solution.py
@@ -141,7 +141,12 @@
         1,
     )
     pair_cols = lax.dynamic_slice_in_dim(
-        lax.all_gather(decode_pairs, ("dp", "head"), axis=0, tiled=True),
+        jnp.concatenate(
+            lax.all_to_all(
+                jnp.stack([decode_pairs] * lax.axis_size(("dp", "head"))), ("dp", "head"), 0, 0
+            ),
+            axis=0,
+        ),
         head_part * pair_width,
         pair_width,
         1,

time: 208 us -> 187 us (0.90)
  blocking collectives: 55.8 us -> 0 us
  waiting for transfers between devices: 19.8 us -> 32.3 us
  starting transfers between devices: 14.6 us -> 26.3 us
  local copies, waits for them, and re-layouts: 41.3 us -> 47.9 us
  other arithmetic: 23.6 us -> 27.6 us
    all_gather x1 -> x0, blocking collectives: 55.8 us -> none  [per_device(): lax.all_gather(decode_pairs, ('dp', 'head'), axis=0, tiled=True)]
    all_to_all x0 -> x1, starting transfers between devices: none -> 10.3 us  [per_device(): lax.all_to_all(jnp.stack([decode_pairs] * lax.axis_size(('dp', 'head'))),...]
    all_to_all x0 -> x1, waiting for transfers between devices: none -> 8.11 us  [per_device(): lax.all_to_all(jnp.stack([decode_pairs] * lax.axis_size(('dp', 'head'))),...]
    all_to_all x1, waiting for transfers between devices: 0.01 us -> 5.53 us  [per_device(): lax.all_to_all(prefill_query, 'head', split_axis=1, concat_axis=0, tiled=...]
    unnamed x22, local copies, waits for them, and re-layouts: 8.98 us -> 13.5 us
    another operation x0 -> x1, other arithmetic: none -> 4 us  [per_device(): jnp.stack([decode_pairs] * lax.axis_size(('dp', 'head')))]
  transfers between devices with their start and end apart: 5 -> 6, of which waited for: 2 -> 3; matrix products, arithmetic and copies ran while one was open for 42% -> 53% of each run, Pallas kernels for 0% -> 0%
where the time goes in v1:
time: 187 us; the launch traced here: 186 us
  local copies, waits for them, and re-layouts  47.9 us (26%)
  matrix products  36.3 us (19%)
  waiting for transfers between devices  32.3 us (17%)
  other arithmetic  27.6 us (15%)
  starting transfers between devices  26.3 us (14%)
  between operations  15.7 us (8%)
    all_to_all x1, waiting for transfers between devices, per_device(): lax.all_to_all(out_span, 'head', split_axis=0, concat_axis=1, tiled=True)  17.9 us
    dot_general x8, matrix products, prefill_block(): jnp.einsum('kqtmp,mkpd->tkqd', weights.astype(jnp.bfloat16), key_pages[.....  16.5 us
    reduce_sum x8, other arithmetic, prefill_block(): weight_sum = jnp.sum(weights, axis=(3, 4))  16.2 us
    unnamed x22, local copies, waits for them, and re-layouts  13.5 us
    dot_general x8, matrix products, prefill_block(): jnp.einsum('tkqd,mkpd->kqtmp', grouped, key_pages[..., :head_size], prefe...  11 us
    all_to_all x1, starting transfers between devices, per_device(): lax.all_to_all(jnp.stack([decode_pairs] * lax.axis_size(('dp', 'head'))),...  10.3 us
    all_to_all x1, waiting for transfers between devices, per_device(): lax.all_to_all(jnp.stack([decode_pairs] * lax.axis_size(('dp', 'head'))),...  8.11 us
    all_to_all x1, starting transfers between devices, per_device(): lax.all_to_all(prefill_pairs, 'head', split_axis=1, concat_axis=0, tiled=...  5.97 us
  transfers between devices with their start and end apart: 6, of which 3 were waited for; matrix products, arithmetic and copies ran while one was open for 53% of the time, Pallas kernels for 0%

profile of v1, /device:TPU:1, one launch (start us, length us, event | category | flops | bytes accessed | tf_op | source)
XLA Modules:
  0.0 186.4 jit_solution(2642213098386185968)
XLA Ops:
  7.3 5.8 %copy.75 = bf16[160,1,64,256]{3,2,1,0:T(8,128)(2,1)} copy(bf16[160,1,64,256]{3,2,1,0:T(8,128)(2,1)} %param.20) | data formatting | bytes 10485760
  13.1 0.7 compare_select_fusion.9
  13.7 0.7 constant_dynamic-slice_fusion.2
  14.4 3.7 %gather_fusion = bf16[4,64,256]{2,1,0:T(8,128)(2,1)} fusion(bf16[160,64,256]{2,1,0:T(8,128)(2,1)} %bitcast.220, s32[1024]{0:T(1024)S(1)} %pad_clamp_fusion.3), kind=kCustom, calls=%fused_computation | custom fusion | bytes 262160 | tf_op jit(solution)/shard_map/gather | solution.py:108
  18.2 0.8 copy.59
  19.0 6.0 %all-to-all-start.2 = ((bf16[128,8,256]{2,0,1:T(8,128)(2,1)}), bf16[128,8,256]{2,0,1:T(8,128)(2,1)S(1)}, u32[]{:S(2)}, u32[]{:S(2)}) async-start(bf16[128,8,256]{2,0,1:T(8,128)(2,1)} %bitcast.187), calls=%async_computation.2 | async-start | bytes 1048576 | tf_op jit(solution)/shard_map/all_to_all | solution.py:166
  25.0 0.7 all-gather.7.cloned.1.call-update
  26.5 0.7 gather_fusion.1
  28.4 4.0 %reduce.10 = bf16[128,2048]{1,0:T(8,128)(2,1)S(1)} reduce(bf16[128,1,2048]{2,1,0:T(2,128)(2,1)S(1)} %stack.2, bf16[]{:T(256)} %broadcast.378), dimensions={1}, to_apply=%stack.2.reduce_sub_computation | reduce | bytes 1048578 | tf_op jit(solution)/shard_map/stack | solution.py:146
  32.4 1.2 reshape.468
  33.6 0.7 fusion.52
  34.3 2.1 %fusion.61 = s32[8]{0:T(128)S(1)} fusion(s32[8]{0:T(128)S(1)} %dynamic_slice.30, s32[]{:T(128)} %bitcast.25, s32[1]{0:T(128)} %bitcast.36, s32[128]{0:T(128)S(1)} %copy-done, s32[]{:T(128)S(6)} %dynamic_slice.31, s32[1,1]{0,1:T(1,128)} %get-tuple-element.67), kind=kLoop, calls=%fused_computation.116 | loop fusion | flops 7 | bytes 560 | tf_op jit(solution)/shard_map/scatter | solution.py:134
  36.4 10.3 %all-to-all-start.1 = ((bf16[128,2,1024]{2,1,0:T(2,128)(2,1)}), bf16[128,2,1024]{2,1,0:T(2,128)(2,1)S(1)}, u32[]{:S(2)}, u32[]{:S(2)}) async-start(bf16[128,2,1024]{2,1,0:T(2,128)(2,1)} %reshape.468), calls=%async_computation.1 | async-start | bytes 1048576 | tf_op jit(solution)/shard_map/all_to_all | solution.py:145
  48.2 4.1 %copy.24 = bf16[128,8192]{0,1:T(8,128)(2,1)} copy(bf16[128,8192]{1,0:T(8,128)(2,1)} %param.16) | data formatting | bytes 4194304 | tf_op args[0]
  52.2 8.1 %all-to-all-done.1 = bf16[128,2,1024]{2,1,0:T(2,128)(2,1)S(1)} async-done(((bf16[128,2,1024]{2,1,0:T(2,128)(2,1)}), bf16[128,2,1024]{2,1,0:T(2,128)(2,1)S(1)}, u32[]{:S(2)}, u32[]{:S(2)}) %all-to-all-start.1) | async-done | bytes 524320 | tf_op jit(solution)/shard_map/all_to_all | solution.py:145
  60.4 5.6 %all-to-all-start = ((bf16[128,8,1024]{0,2,1:T(8,128)(2,1)}), bf16[128,8,1024]{0,2,1:T(8,128)(2,1)S(1)}, u32[]{:S(2)}, u32[]{:S(2)}) async-start(bf16[128,8,1024]{0,2,1:T(8,128)(2,1)} %bitcast.21), calls=%async_computation | async-start | bytes 4194304 | tf_op jit(solution)/shard_map/all_to_all | solution.py:165
  66.1 1.7 reshape.469
  67.9 1.0 constant_dynamic-slice_fusion.5
  69.1 2.9 %fusion.27 = bf16[1,4,64,256]{3,0,2,1:T(2,128)(2,1)S(1)} fusion(bf16[16,4,64,256]{3,2,1,0:T(8,128)(2,1)} %bitcast.229, s32[16,1]{0,1:T(1,128)S(1)} %copy-done.4, s32[]{:T(128)S(6)} %axis_index.23), kind=kOutput, calls=%fused_computation.38 | convolution fusion | flops 2097168 | bytes 2228292 | tf_op jit(solution)/shard_map/nk,nabcd->kabcd/dot_general | solution.py:117
  72.0 2.0 %scatter_fusion = bf16[160,64,256]{2,1,0:T(8,128)(2,1)} fusion(bf16[160,64,256]{2,1,0:T(8,128)(2,1)} %bitcast.221, s32[4]{0:T(128)S(1)} %fusion.54, bf16[4,64,256]{2,1,0:T(8,128)(2,1)S(1)} %bitcast.231), kind=kCustom, calls=%fused_computation.5 | custom fusion | bytes 393232 | tf_op jit(solution)/shard_map/scatter | solution.py:124
  74.0 2.1 %scatter_fusion.1 = bf16[160,64,256]{2,1,0:T(8,128)(2,1)} fusion(bf16[160,64,256]{2,1,0:T(8,128)(2,1)} %scatter_fusion, s32[8]{0:T(128)S(1)} %fusion.62, bf16[8,256]{1,0:T(8,128)(2,1)S(1)} %convolution_convert_fusion.1), kind=kCustom, calls=%fused_computation.6 | custom fusion | bytes 12352 | tf_op jit(solution)/shard_map/scatter | solution.py:160
  76.1 5.3 %gather_fusion.3 = bf16[128,64,256]{2,1,0:T(8,128)(2,1)} fusion(bf16[160,64,256]{2,1,0:T(8,128)(2,1)} %scatter_fusion.1, s32[1024]{0:T(1024)S(1)} %pad_clamp_fusion), kind=kCustom, calls=%fused_computation.3 | custom fusion | bytes 8389120 | tf_op jit(solution)/shard_map/gather | solution.py:163
  81.4 2.6 %scatter_fusion.2 = bf16[160,64,256]{2,1,0:T(8,128)(2,1)} fusion(bf16[160,64,256]{2,1,0:T(8,128)(2,1)} %scatter_fusion.1, s32[16]{0:T(128)S(1)} %fusion.60, bf16[16,64,256]{2,1,0:T(8,128)(2,1)S(1)} %bitcast.230), kind=kCustom, calls=%fused_computation.7 | custom fusion | bytes 1572928 | tf_op jit(solution)/shard_map/scatter | solution.py:175
  83.9 3.1 %gather_fusion.2 = bf16[32,64,256]{2,1,0:T(8,128)(2,1)S(1)} fusion(bf16[160,64,256]{2,1,0:T(8,128)(2,1)} %scatter_fusion.2, s32[1024]{0:T(1024)S(1)} %pad_clamp_fusion.1), kind=kCustom, calls=%fused_computation.2 | custom fusion | bytes 2097280 | tf_op jit(solution)/shard_map/gather | solution.py:176
  87.0 5.5 %all-to-all-done = bf16[128,8,1024]{0,2,1:T(8,128)(2,1)S(1)} async-done(((bf16[128,8,1024]{0,2,1:T(8,128)(2,1)}), bf16[128,8,1024]{0,2,1:T(8,128)(2,1)S(1)}, u32[]{:S(2)}, u32[]{:S(2)}) %all-to-all-start) | async-done | bytes 2097184 | tf_op jit(solution)/shard_map/all_to_all | solution.py:165
  92.6 53.4 %while.12 = (s32[]{:T(128)}, bf16[8,128,1024]{1,2,0:T(8,128)(2,1)}, s32[8,128]{1,0:T(8,128)S(1)}, bf16[8,128,1024]{1,2,0:T(8,128)(2,1)S(1)}, bf16[32,1,64,256]{3,2,0,1:T(8,128)(2,1)S(1)}, /*index=5*/s32[]{:T(128)}) while((s32[]{:T(128)}, bf16[8,128,1024]{1,2,0:T(8,128)(2,1)}, s32[8,128]{1,0:T(8,128)S(1)}, bf16[8,128,1024]{1,2,0:T(8,128)(2,1)S(1)}, ...), condition=%wide.region_7.8_spmd, body=%wide.region_4.7_spmd.sunk | while | flops 1101529088 | bytes 28875084 | solution.py:186
  93.0 1.4 fusion.79
  94.4 2.0 %fusion.80 = f32[8,128]{1,0:T(8,128)S(1)} fusion(f32[128,8,32,64]{0,3,2,1:T(8,128)S(1)} %get-tuple-element.103, f32[8,128]{1,0:T(8,128)S(1)} %get-tuple-element.104, pred[128,32,64]{0,2,1:T(8,128)(4,1)S(1)} %broadcast_compare_fusion.3), kind=kLoop, calls=%fused_computation.11.clone.1 | loop fusion | flops 10484736 | bytes 8658944 | tf_op jit(solution)/shard_map/while/body/eval_jaxpr/reduce_sum | solution.py:70
  96.4 2.1 %fusion.81 = bf16[128,1,8,128]{0,3,2,1:T(8,128)(2,1)S(1)} fusion(f32[128,8,32,64]{0,3,2,1:T(8,128)S(1)} %get-tuple-element.103, f32[8,128]{1,0:T(8,128)S(1)} %get-tuple-element.104, pred[128,32,64]{0,2,1:T(8,128)(4,1)S(1)} %broadcast_compare_fusion.3, bf16[32,1,64,256]{3,2,0,1:T(8,128)(2,1)S(1)} %get-tuple-element.121, f32[128,8]{0,1:T(8,128)S(1)} %bitcast.233), kind=kOutput, calls=%fused_computation.18.clone.1 | convolution fusion | flops 547618816 | bytes 9445376 | tf_op jit(solution)/shard_map/while/body/eval_jaxpr/kqtmp,mkpd->tkqd/dot_general | solution.py:71
  98.5 0.7 constant_dynamic-update-slice_fusion.2
  99.7 1.4 fusion.79
  101.1 2.0 %fusion.80 = f32[8,128]{1,0:T(8,128)S(1)} fusion(f32[128,8,32,64]{0,3,2,1:T(8,128)S(1)} %get-tuple-element.103, f32[8,128]{1,0:T(8,128)S(1)} %get-tuple-element.104, pred[128,32,64]{0,2,1:T(8,128)(4,1)S(1)} %broadcast_compare_fusion.3), kind=kLoop, calls=%fused_computation.11.clone.1 | loop fusion | flops 10484736 | bytes 8658944 | tf_op jit(solution)/shard_map/while/body/eval_jaxpr/reduce_sum | solution.py:70
  103.1 2.1 %fusion.81 = bf16[128,1,8,128]{0,3,2,1:T(8,128)(2,1)S(1)} fusion(f32[128,8,32,64]{0,3,2,1:T(8,128)S(1)} %get-tuple-element.103, f32[8,128]{1,0:T(8,128)S(1)} %get-tuple-element.104, pred[128,32,64]{0,2,1:T(8,128)(4,1)S(1)} %broadcast_compare_fusion.3, bf16[32,1,64,256]{3,2,0,1:T(8,128)(2,1)S(1)} %get-tuple-element.121, f32[128,8]{0,1:T(8,128)S(1)} %bitcast.233), kind=kOutput, calls=%fused_computation.18.clone.1 | convolution fusion | flops 547618816 | bytes 9445376 | tf_op jit(solution)/shard_map/while/body/eval_jaxpr/kqtmp,mkpd->tkqd/dot_general | solution.py:71
  105.2 0.7 constant_dynamic-update-slice_fusion.2
  106.4 1.4 fusion.79
  107.8 2.0 %fusion.80 = f32[8,128]{1,0:T(8,128)S(1)} fusion(f32[128,8,32,64]{0,3,2,1:T(8,128)S(1)} %get-tuple-element.103, f32[8,128]{1,0:T(8,128)S(1)} %get-tuple-element.104, pred[128,32,64]{0,2,1:T(8,128)(4,1)S(1)} %broadcast_compare_fusion.3), kind=kLoop, calls=%fused_computation.11.clone.1 | loop fusion | flops 10484736 | bytes 8658944 | tf_op jit(solution)/shard_map/while/body/eval_jaxpr/reduce_sum | solution.py:70
  109.8 2.1 %fusion.81 = bf16[128,1,8,128]{0,3,2,1:T(8,128)(2,1)S(1)} fusion(f32[128,8,32,64]{0,3,2,1:T(8,128)S(1)} %get-tuple-element.103, f32[8,128]{1,0:T(8,128)S(1)} %get-tuple-element.104, pred[128,32,64]{0,2,1:T(8,128)(4,1)S(1)} %broadcast_compare_fusion.3, bf16[32,1,64,256]{3,2,0,1:T(8,128)(2,1)S(1)} %get-tuple-element.121, f32[128,8]{0,1:T(8,128)S(1)} %bitcast.233), kind=kOutput, calls=%fused_computation.18.clone.1 | convolution fusion | flops 547618816 | bytes 9445376 | tf_op jit(solution)/shard_map/while/body/eval_jaxpr/kqtmp,mkpd->tkqd/dot_general | solution.py:71
  111.9 0.7 constant_dynamic-update-slice_fusion.2
  113.1 1.4 fusion.79
  114.4 2.0 %fusion.80 = f32[8,128]{1,0:T(8,128)S(1)} fusion(f32[128,8,32,64]{0,3,2,1:T(8,128)S(1)} %get-tuple-element.103, f32[8,128]{1,0:T(8,128)S(1)} %get-tuple-element.104, pred[128,32,64]{0,2,1:T(8,128)(4,1)S(1)} %broadcast_compare_fusion.3), kind=kLoop, calls=%fused_computation.11.clone.1 | loop fusion | flops 10484736 | bytes 8658944 | tf_op jit(solution)/shard_map/while/body/eval_jaxpr/reduce_sum | solution.py:70
  116.5 2.1 %fusion.81 = bf16[128,1,8,128]{0,3,2,1:T(8,128)(2,1)S(1)} fusion(f32[128,8,32,64]{0,3,2,1:T(8,128)S(1)} %get-tuple-element.103, f32[8,128]{1,0:T(8,128)S(1)} %get-tuple-element.104, pred[128,32,64]{0,2,1:T(8,128)(4,1)S(1)} %broadcast_compare_fusion.3, bf16[32,1,64,256]{3,2,0,1:T(8,128)(2,1)S(1)} %get-tuple-element.121, f32[128,8]{0,1:T(8,128)S(1)} %bitcast.233), kind=kOutput, calls=%fused_computation.18.clone.1 | convolution fusion | flops 547618816 | bytes 9445376 | tf_op jit(solution)/shard_map/while/body/eval_jaxpr/kqtmp,mkpd->tkqd/dot_general | solution.py:71
  118.5 0.7 constant_dynamic-update-slice_fusion.2
  119.7 1.4 fusion.79
  121.1 2.0 %fusion.80 = f32[8,128]{1,0:T(8,128)S(1)} fusion(f32[128,8,32,64]{0,3,2,1:T(8,128)S(1)} %get-tuple-element.103, f32[8,128]{1,0:T(8,128)S(1)} %get-tuple-element.104, pred[128,32,64]{0,2,1:T(8,128)(4,1)S(1)} %broadcast_compare_fusion.3), kind=kLoop, calls=%fused_computation.11.clone.1 | loop fusion | flops 10484736 | bytes 8658944 | tf_op jit(solution)/shard_map/while/body/eval_jaxpr/reduce_sum | solution.py:70
  123.1 2.1 %fusion.81 = bf16[128,1,8,128]{0,3,2,1:T(8,128)(2,1)S(1)} fusion(f32[128,8,32,64]{0,3,2,1:T(8,128)S(1)} %get-tuple-element.103, f32[8,128]{1,0:T(8,128)S(1)} %get-tuple-element.104, pred[128,32,64]{0,2,1:T(8,128)(4,1)S(1)} %broadcast_compare_fusion.3, bf16[32,1,64,256]{3,2,0,1:T(8,128)(2,1)S(1)} %get-tuple-element.121, f32[128,8]{0,1:T(8,128)S(1)} %bitcast.233), kind=kOutput, calls=%fused_computation.18.clone.1 | convolution fusion | flops 547618816 | bytes 9445376 | tf_op jit(solution)/shard_map/while/body/eval_jaxpr/kqtmp,mkpd->tkqd/dot_general | solution.py:71
  125.2 0.7 constant_dynamic-update-slice_fusion.2
  126.4 1.4 fusion.79
  127.8 2.0 %fusion.80 = f32[8,128]{1,0:T(8,128)S(1)} fusion(f32[128,8,32,64]{0,3,2,1:T(8,128)S(1)} %get-tuple-element.103, f32[8,128]{1,0:T(8,128)S(1)} %get-tuple-element.104, pred[128,32,64]{0,2,1:T(8,128)(4,1)S(1)} %broadcast_compare_fusion.3), kind=kLoop, calls=%fused_computation.11.clone.1 | loop fusion | flops 10484736 | bytes 8658944 | tf_op jit(solution)/shard_map/while/body/eval_jaxpr/reduce_sum | solution.py:70
  129.8 2.1 %fusion.81 = bf16[128,1,8,128]{0,3,2,1:T(8,128)(2,1)S(1)} fusion(f32[128,8,32,64]{0,3,2,1:T(8,128)S(1)} %get-tuple-element.103, f32[8,128]{1,0:T(8,128)S(1)} %get-tuple-element.104, pred[128,32,64]{0,2,1:T(8,128)(4,1)S(1)} %broadcast_compare_fusion.3, bf16[32,1,64,256]{3,2,0,1:T(8,128)(2,1)S(1)} %get-tuple-element.121, f32[128,8]{0,1:T(8,128)S(1)} %bitcast.233), kind=kOutput, calls=%fused_computation.18.clone.1 | convolution fusion | flops 547618816 | bytes 9445376 | tf_op jit(solution)/shard_map/while/body/eval_jaxpr/kqtmp,mkpd->tkqd/dot_general | solution.py:71
  131.9 0.7 constant_dynamic-update-slice_fusion.2
  133.1 1.4 fusion.79
  134.5 2.0 %fusion.80 = f32[8,128]{1,0:T(8,128)S(1)} fusion(f32[128,8,32,64]{0,3,2,1:T(8,128)S(1)} %get-tuple-element.103, f32[8,128]{1,0:T(8,128)S(1)} %get-tuple-element.104, pred[128,32,64]{0,2,1:T(8,128)(4,1)S(1)} %broadcast_compare_fusion.3), kind=kLoop, calls=%fused_computation.11.clone.1 | loop fusion | flops 10484736 | bytes 8658944 | tf_op jit(solution)/shard_map/while/body/eval_jaxpr/reduce_sum | solution.py:70
  136.5 2.1 %fusion.81 = bf16[128,1,8,128]{0,3,2,1:T(8,128)(2,1)S(1)} fusion(f32[128,8,32,64]{0,3,2,1:T(8,128)S(1)} %get-tuple-element.103, f32[8,128]{1,0:T(8,128)S(1)} %get-tuple-element.104, pred[128,32,64]{0,2,1:T(8,128)(4,1)S(1)} %broadcast_compare_fusion.3, bf16[32,1,64,256]{3,2,0,1:T(8,128)(2,1)S(1)} %get-tuple-element.121, f32[128,8]{0,1:T(8,128)S(1)} %bitcast.233), kind=kOutput, calls=%fused_computation.18.clone.1 | convolution fusion | flops 547618816 | bytes 9445376 | tf_op jit(solution)/shard_map/while/body/eval_jaxpr/kqtmp,mkpd->tkqd/dot_general | solution.py:71
  138.6 0.7 constant_dynamic-update-slice_fusion.2
  139.7 1.4 fusion.79
  141.1 2.0 %fusion.80 = f32[8,128]{1,0:T(8,128)S(1)} fusion(f32[128,8,32,64]{0,3,2,1:T(8,128)S(1)} %get-tuple-element.103, f32[8,128]{1,0:T(8,128)S(1)} %get-tuple-element.104, pred[128,32,64]{0,2,1:T(8,128)(4,1)S(1)} %broadcast_compare_fusion.3), kind=kLoop, calls=%fused_computation.11.clone.1 | loop fusion | flops 10484736 | bytes 8658944 | tf_op jit(solution)/shard_map/while/body/eval_jaxpr/reduce_sum | solution.py:70
  143.2 2.1 %fusion.81 = bf16[128,1,8,128]{0,3,2,1:T(8,128)(2,1)S(1)} fusion(f32[128,8,32,64]{0,3,2,1:T(8,128)S(1)} %get-tuple-element.103, f32[8,128]{1,0:T(8,128)S(1)} %get-tuple-element.104, pred[128,32,64]{0,2,1:T(8,128)(4,1)S(1)} %broadcast_compare_fusion.3, bf16[32,1,64,256]{3,2,0,1:T(8,128)(2,1)S(1)} %get-tuple-element.121, f32[128,8]{0,1:T(8,128)S(1)} %bitcast.233), kind=kOutput, calls=%fused_computation.18.clone.1 | convolution fusion | flops 547618816 | bytes 9445376 | tf_op jit(solution)/shard_map/while/body/eval_jaxpr/kqtmp,mkpd->tkqd/dot_general | solution.py:71
  145.2 0.7 constant_dynamic-update-slice_fusion.2
  146.0 4.4 %all-to-all-start.3 = ((bf16[8,128,1024]{1,2,0:T(8,128)(2,1)}), bf16[8,128,1024]{1,2,0:T(8,128)(2,1)S(1)}, u32[]{:S(2)}, u32[]{:S(2)}) async-start(bf16[8,128,1024]{1,2,0:T(8,128)(2,1)} %get-tuple-element.42), calls=%async_computation.3 | async-start | bytes 4194304 | tf_op jit(solution)/shard_map/all_to_all | solution.py:188
  150.5 1.6 constant_dynamic-slice_fusion.3
  152.3 3.4 %fusion.65 = (f32[8,8]{1,0:T(8,128)S(1)}, f32[8,8,16,64]{3,1,2,0:T(8,128)S(1)}) fusion(bf16[8,16,1,64,256]{4,3,1,0,2:T(8,128)(2,1)} %bitcast.224, bf16[8,8,128,1]{2,0,1,3:T(8,128)(2,1)S(1)} %fusion.32, pred[8,16,64]{2,1,0:T(8,128)(4,1)S(1)} %broadcast_compare_fusion.1), kind=kOutput, calls=%fused_computation.120 | convolution fusion | flops 16973760 | bytes 2384128 | tf_op jit(solution)/shard_map/skqd,smkpd->skqmp/dot_general | solution.py:20
  156.0 2.2 %fusion.35 = bf16[1,8,8,128]{3,2,1,0:T(8,128)(2,1)S(1)} fusion(bf16[8,16,1,64,256]{4,3,1,0,2:T(8,128)(2,1)} %bitcast.225, f32[8,8,16,64]{3,1,2,0:T(8,128)S(1)} %get-tuple-element.69, f32[8,8]{1,0:T(8,128)S(1)} %get-tuple-element.68, pred[8,16,64]{2,1,0:T(8,128)(4,1)S(1)} %broadcast_compare_fusion.1, f32[8,8]{1,0:T(8,128)S(1)} %fusion.36), kind=kOutput, calls=%fused_computation.48 | convolution fusion | flops 16990208 | bytes 2384384 | tf_op jit(solution)/shard_map/skqmp,smkpd->skqd/dot_general | solution.py:37
  158.8 17.9 %all-to-all-done.3 = bf16[8,128,1024]{1,2,0:T(8,128)(2,1)S(1)} async-done(((bf16[8,128,1024]{1,2,0:T(8,128)(2,1)}), bf16[8,128,1024]{1,2,0:T(8,128)(2,1)S(1)}, u32[]{:S(2)}, u32[]{:S(2)}) %all-to-all-start.3) | async-done | bytes 2097184 | tf_op jit(solution)/shard_map/all_to_all | solution.py:188
  176.7 2.9 %copy.39 = bf16[128,8192]{1,0:T(8,128)(2,1)} copy(bf16[128,8192]{0,1:T(8,128)(2,1)S(1)} %bitcast.226) | data formatting | bytes 4194304 | tf_op jit(solution)/shard_map/all_to_all | solution.py:188
  (94 shorter events, 7.3 us)
Async XLA Ops:
  7.2 11.0 %copy-start.2 = (bf16[128,2048]{1,0:T(8,128)(2,1)S(1)}, bf16[128,2048]{1,0:T(8,128)(2,1)}, u32[]{:S(2)}) copy-start(bf16[128,2048]{1,0:T(8,128)(2,1)} %param.17) | copy-start | bytes 1572868
  7.2 20.0 %copy-start.3 = (bf16[1,2048]{1,0:T(2,128)(2,1)S(1)}, bf16[1,2048]{1,0:T(2,128)(2,1)}, u32[]{:S(2)}) copy-start(bf16[1,2048]{1,0:T(2,128)(2,1)} %param.19) | copy-start | bytes 12292
  7.2 6.5 %copy-start.1 = (s32[8,16]{1,0:T(8,128)S(1)}, s32[8,16]{1,0:T(8,128)}, u32[]{:S(2)}) copy-start(s32[8,16]{1,0:T(8,128)} %param.21) | copy-start | bytes 1540
  7.2 19.2 %copy-start = (s32[128]{0:T(128)S(1)}, s32[128]{0:T(128)}, u32[]{:S(2)}) copy-start(s32[128]{0:T(128)} %param.23) | copy-start | bytes 1540
  7.2 5.9 %copy-start.5 = (s32[16,1]{0,1:T(1,128)S(1)}, s32[16,1]{0,1:T(1,128)}, u32[]{:S(2)}) copy-start(s32[16,1]{0,1:T(1,128)} %param.25) | copy-start | bytes 196
  7.2 61.9 %all-gather.5.cloned.1.call-start = ((), (), s32[]{:S(2)}) async-start(), calls=%async_computation.4 | async-start | bytes 2228224 | tf_op jit(solution)/shard_map/all_gather | solution.py:110
  13.1 20.5 %copy-start.4 = (s32[16,1]{0,1:T(1,128)S(1)}, s32[16,1]{0,1:T(1,128)}, u32[]{:S(2)}) copy-start(s32[16,1]{0,1:T(1,128)} %param.26) | copy-start | bytes 196
  19.0 17.4 %all-to-all-start.2 = ((bf16[128,8,256]{2,0,1:T(8,128)(2,1)}), bf16[128,8,256]{2,0,1:T(8,128)(2,1)S(1)}, u32[]{:S(2)}, u32[]{:S(2)}) async-start(bf16[128,8,256]{2,0,1:T(8,128)(2,1)} %bitcast.187), calls=%async_computation.2 | async-start | bytes 1048576 | tf_op jit(solution)/shard_map/all_to_all | solution.py:166
  25.0 125.6 %all-gather.7.cloned.1.call-start = ((), (), s32[]{:S(2)}) async-start(), calls=%async_computation.5 | async-start | bytes 4227072 | tf_op jit(solution)/shard_map/all_gather | solution.py:138
  33.6 32.4 %copy-start.6 = (s32[1,32]{1,0:T(1,128)S(1)}, s32[1,32]{1,0:T(1,128)}, u32[]{:S(2)}) copy-start(s32[1,32]{1,0:T(1,128)} %param.22) | copy-start | bytes 388
  36.4 24.0 %all-to-all-start.1 = ((bf16[128,2,1024]{2,1,0:T(2,128)(2,1)}), bf16[128,2,1024]{2,1,0:T(2,128)(2,1)S(1)}, u32[]{:S(2)}, u32[]{:S(2)}) async-start(bf16[128,2,1024]{2,1,0:T(2,128)(2,1)} %reshape.468), calls=%async_computation.1 | async-start | bytes 1048576 | tf_op jit(solution)/shard_map/all_to_all | solution.py:145
  47.4 21.5 %copy-start.7 = (s32[128]{0:T(128)S(1)}, s32[128]{0:T(128)}, u32[]{:S(2)}) copy-start(s32[128]{0:T(128)} %param.27) | copy-start | bytes 1540
  60.4 32.2 %all-to-all-start = ((bf16[128,8,1024]{0,2,1:T(8,128)(2,1)}), bf16[128,8,1024]{0,2,1:T(8,128)(2,1)S(1)}, u32[]{:S(2)}, u32[]{:S(2)}) async-start(bf16[128,8,1024]{0,2,1:T(8,128)(2,1)} %bitcast.21), calls=%async_computation | async-start | bytes 4194304 | tf_op jit(solution)/shard_map/all_to_all | solution.py:165
  146.0 30.7 %all-to-all-start.3 = ((bf16[8,128,1024]{1,2,0:T(8,128)(2,1)}), bf16[8,128,1024]{1,2,0:T(8,128)(2,1)S(1)}, u32[]{:S(2)}, u32[]{:S(2)}) async-start(bf16[8,128,1024]{1,2,0:T(8,128)(2,1)} %get-tuple-element.42), calls=%async_computation.3 | async-start | bytes 4194304 | tf_op jit(solution)/shard_map/all_to_all | solution.py:188
Sparse Core Ops, SparseCore 0:
  18.3 49.7 all-gather.4
  71.2 66.4 all-gather.6
